TPU v7x, 32 devices: a whole 2x2x4 slice. The times are simulated.
32 devices in a mesh: fsdp: 32 (over z, y, x, core).
Axes of the slice: x: 2, y: 2, z: 4, core: 2. Of those that a mesh axis runs over, the one named last changes fastest.
Arguments:
- layer_input: bfloat16 [96, 288, 768], P('fsdp'), may hold values from -6 to 6
- segments: int32 [96, 288], P('fsdp'), may hold values from 0 to 8, as said below
- cotangent: bfloat16 [96, 288, 768], P('fsdp'), may hold values from -6 to 6
- pre_gain: float32 [768], P('fsdp'), may hold values from 0.5 to 1.5
- pre_shift: float32 [768], P('fsdp'), may hold values from -2 to 2
- w_qkv: float32 [768, 2304], P('fsdp'), may hold values from -0.21875 to 0.21875
- b_query: float32 [768], P('fsdp'), may hold values from -3 to 3
- b_value: float32 [768], P('fsdp'), may hold values from -3 to 3
- w_out: float32 [768, 768], P('fsdp'), may hold values from -1.25 to 1.25
- b_out: float32 [768], P('fsdp'), may hold values from -3 to 3
- mid_gain: float32 [768], P('fsdp'), may hold values from 0.5 to 1.5
- mid_shift: float32 [768], P('fsdp'), may hold values from -2 to 2
- w_up: float32 [768, 3072], P('fsdp'), may hold values from -0.21875 to 0.21875
- b_up: float32 [3072], P('fsdp'), may hold values from -3 to 3
- w_down: float32 [3072, 768], P('fsdp'), may hold values from -0.109375 to 0.109375
- b_down: float32 [768], P('fsdp'), may hold values from -3 to 3
Outputs:
- layer_output: bfloat16 [96, 288, 768], P('fsdp')
- grad_input: bfloat16 [96, 288, 768], P('fsdp')
- grad_pre_gain: float32 [768], P('fsdp')
- grad_pre_shift: float32 [768], P('fsdp')
- grad_w_qkv: float32 [768, 2304], P('fsdp')
- grad_b_query: float32 [768], P('fsdp')
- grad_b_value: float32 [768], P('fsdp')
- grad_w_out: float32 [768, 768], P('fsdp')
- grad_b_out: float32 [768], P('fsdp')
- grad_mid_gain: float32 [768], P('fsdp')
- grad_mid_shift: float32 [768], P('fsdp')
- grad_w_up: float32 [768, 3072], P('fsdp')
- grad_b_up: float32 [3072], P('fsdp')
- grad_w_down: float32 [3072, 768], P('fsdp')
- grad_b_down: float32 [768], P('fsdp')
Inputs may be any that keep to these rules, and one draw needn't show every extreme that they name: `segments`: each row holds 8 or 7 images of 36 slots each, in slot order and numbered from 1; the remaining slots of a row are padding (0).
All inputs are finite; a program needn't handle non-finite values.
Results may differ from a plain program's by a relative error of at most 0.012.
The roundings to bfloat16 on the way count: a program that leaves them out, or rounds other values in their place, can miss the bound.
Values may be sent and summed in bfloat16 or wider, within the bound.
No kernel may reach another device: no remote copies, remote signals or barrier semaphores. Data moves between devices by JAX's collectives and lax.ppermute only.
A program may use at most 192 MiB of HBM per device.

v0:
```python
import jax
import jax.numpy as jnp
from jax import lax
from jax.sharding import PartitionSpec as P

HEAD_DIM = 64
PATCHES = 36
EPSILON = 1e-06


def norm_layer(value, gain, shift):
    average = jnp.mean(value, axis=-1, keepdims=True)
    centred = value - average
    spread = jnp.mean(centred * centred, axis=-1, keepdims=True)
    return centred * lax.rsqrt(spread + EPSILON) * gain + shift


def gelu_exact(value):
    return jax.nn.gelu(value, approximate=False)


def column_sums(value):
    return jnp.sum(value.astype(jnp.float32), axis=0)


def shards(
    layer_input,
    segments,
    cotangent,
    pre_gain,
    pre_shift,
    w_qkv,
    b_query,
    b_value,
    w_out,
    b_out,
    mid_gain,
    mid_shift,
    w_up,
    b_up,
    w_down,
    b_down,
):
    row_count, slot_count, model_width = layer_input.shape
    head_count = model_width // HEAD_DIM
    tokens = row_count * slot_count
    images = slot_count // PATCHES
    scaling = HEAD_DIM ** (-0.5)
    tiled = (row_count, images, PATCHES, head_count, HEAD_DIM)
    attn_full = (
        lax.all_gather(pre_gain.astype(jnp.bfloat16), "fsdp", axis=0, tiled=True),
        lax.all_gather(pre_shift.astype(jnp.bfloat16), "fsdp", axis=0, tiled=True),
        lax.all_gather(w_qkv.astype(jnp.bfloat16), "fsdp", axis=0, tiled=True),
        lax.all_gather(b_query.astype(jnp.bfloat16), "fsdp", axis=0, tiled=True),
        lax.all_gather(b_value.astype(jnp.bfloat16), "fsdp", axis=0, tiled=True),
        lax.all_gather(w_out.astype(jnp.bfloat16), "fsdp", axis=0, tiled=True),
        lax.all_gather(b_out.astype(jnp.bfloat16), "fsdp", axis=0, tiled=True),
    )
    gain_one, shift_one, qkv_weight, query_bias, value_bias, out_weight, out_bias = attn_full
    inputs = layer_input.astype(jnp.float32).reshape(tokens, model_width)
    normed_one, norm_back_one = jax.vjp(
        norm_layer, inputs, gain_one.astype(jnp.float32), shift_one.astype(jnp.float32)
    )
    first = normed_one.astype(jnp.bfloat16)
    qkv_bias = jnp.concatenate(
        [
            query_bias.astype(jnp.float32),
            jnp.zeros((model_width,), jnp.float32),
            value_bias.astype(jnp.float32),
        ]
    )
    qkv = (jnp.dot(first, qkv_weight, preferred_element_type=jnp.float32) + qkv_bias).astype(
        jnp.bfloat16
    )
    queries = qkv[:, :model_width].reshape(tiled)
    key_heads = qkv[:, model_width : 2 * model_width].reshape(tiled)
    value_heads = qkv[:, 2 * model_width :].reshape(tiled)
    image_segs = segments.reshape(row_count, images, PATCHES)
    matching = image_segs[:, :, :, None] == image_segs[:, :, None, :]
    occupied = (image_segs > 0)[:, :, :, None]
    diagonal = (
        lax.broadcasted_iota(jnp.int32, (PATCHES, PATCHES), 0)
        == lax.broadcasted_iota(jnp.int32, (PATCHES, PATCHES), 1)
    )[None, None]
    allowed = (matching & occupied | diagonal)[:, :, None]

    def masked_scores():
        raw = (
            jnp.einsum("rnqhe,rnkhe->rnhqk", queries, key_heads, preferred_element_type=jnp.float32)
            * scaling
        )
        return jnp.where(allowed, raw, -1000000000.0)

    scores = masked_scores()
    highest = jnp.max(scores, axis=-1, keepdims=True)
    log_total = highest + jnp.log(jnp.sum(jnp.exp(scores - highest), axis=-1, keepdims=True))
    probs_low = jnp.exp(scores - log_total).astype(jnp.bfloat16)
    context = jnp.einsum(
        "rnhqk,rnkhe->rnqhe", probs_low, value_heads, preferred_element_type=jnp.float32
    )
    context_low = context.reshape(tokens, model_width).astype(jnp.bfloat16)
    attention = jnp.dot(
        context_low, out_weight, preferred_element_type=jnp.float32
    ) + out_bias.astype(jnp.float32)
    middle = inputs + attention
    mlp_full = (
        lax.all_gather(mid_gain.astype(jnp.bfloat16), "fsdp", axis=0, tiled=True),
        lax.all_gather(mid_shift.astype(jnp.bfloat16), "fsdp", axis=0, tiled=True),
        lax.all_gather(w_up.astype(jnp.bfloat16), "fsdp", axis=0, tiled=True),
        lax.all_gather(b_up.astype(jnp.bfloat16), "fsdp", axis=0, tiled=True),
        lax.all_gather(w_down.astype(jnp.bfloat16), "fsdp", axis=0, tiled=True),
        lax.all_gather(b_down.astype(jnp.bfloat16), "fsdp", axis=0, tiled=True),
    )
    gain_two, shift_two, up_weight, up_bias, down_weight, down_bias = mlp_full
    normed_two, norm_back_two = jax.vjp(
        norm_layer, middle, gain_two.astype(jnp.float32), shift_two.astype(jnp.float32)
    )
    second = normed_two.astype(jnp.bfloat16)
    hidden = jnp.dot(second, up_weight, preferred_element_type=jnp.float32) + up_bias.astype(
        jnp.float32
    )
    activated, gelu_back = jax.vjp(gelu_exact, hidden)
    activated_low = activated.astype(jnp.bfloat16)
    branch = jnp.dot(
        activated_low, down_weight, preferred_element_type=jnp.float32
    ) + down_bias.astype(jnp.float32)
    result = (middle + branch).astype(jnp.bfloat16).reshape(row_count, slot_count, model_width)
    mlp_back = (
        lax.all_gather(mid_gain.astype(jnp.bfloat16), "fsdp", axis=0, tiled=True),
        lax.all_gather(mid_shift.astype(jnp.bfloat16), "fsdp", axis=0, tiled=True),
        lax.all_gather(w_up.astype(jnp.bfloat16), "fsdp", axis=0, tiled=True),
        lax.all_gather(b_up.astype(jnp.bfloat16), "fsdp", axis=0, tiled=True),
        lax.all_gather(w_down.astype(jnp.bfloat16), "fsdp", axis=0, tiled=True),
        lax.all_gather(b_down.astype(jnp.bfloat16), "fsdp", axis=0, tiled=True),
    )
    up_again, down_again = (mlp_back[2], mlp_back[4])
    upstream = cotangent.astype(jnp.float32).reshape(tokens, model_width)
    grad_branch = cotangent.reshape(tokens, model_width)
    grad_down = jnp.einsum(
        "tf,td->fd", activated_low, grad_branch, preferred_element_type=jnp.float32
    )
    grad_down_bias = column_sums(grad_branch)
    grad_act = jnp.einsum("td,fd->tf", grad_branch, down_again, preferred_element_type=jnp.float32)
    grad_hidden = gelu_back(grad_act)[0].astype(jnp.bfloat16)
    grad_up = jnp.einsum("td,tf->df", second, grad_hidden, preferred_element_type=jnp.float32)
    grad_up_bias = column_sums(grad_hidden)
    grad_second = jnp.einsum("tf,df->td", grad_hidden, up_again, preferred_element_type=jnp.float32)
    grad_mid_norm, grad_gain_two, grad_shift_two = norm_back_two(grad_second)
    grad_middle = upstream + grad_mid_norm
    mlp_sums = (
        lax.psum_scatter(grad_gain_two, "fsdp", scatter_dimension=0, tiled=True),
        lax.psum_scatter(grad_shift_two, "fsdp", scatter_dimension=0, tiled=True),
        lax.psum_scatter(grad_up, "fsdp", scatter_dimension=0, tiled=True),
        lax.psum_scatter(grad_up_bias, "fsdp", scatter_dimension=0, tiled=True),
        lax.psum_scatter(grad_down, "fsdp", scatter_dimension=0, tiled=True),
        lax.psum_scatter(grad_down_bias, "fsdp", scatter_dimension=0, tiled=True),
    )
    attn_back = (
        lax.all_gather(pre_gain.astype(jnp.bfloat16), "fsdp", axis=0, tiled=True),
        lax.all_gather(pre_shift.astype(jnp.bfloat16), "fsdp", axis=0, tiled=True),
        lax.all_gather(w_qkv.astype(jnp.bfloat16), "fsdp", axis=0, tiled=True),
        lax.all_gather(b_query.astype(jnp.bfloat16), "fsdp", axis=0, tiled=True),
        lax.all_gather(b_value.astype(jnp.bfloat16), "fsdp", axis=0, tiled=True),
        lax.all_gather(w_out.astype(jnp.bfloat16), "fsdp", axis=0, tiled=True),
        lax.all_gather(b_out.astype(jnp.bfloat16), "fsdp", axis=0, tiled=True),
    )
    qkv_again, out_again = (attn_back[2], attn_back[5])
    grad_attention = grad_middle.astype(jnp.bfloat16)
    grad_out = jnp.einsum(
        "ti,to->io", context_low, grad_attention, preferred_element_type=jnp.float32
    )
    grad_out_bias = column_sums(grad_attention)
    grad_context = jnp.einsum(
        "to,io->ti", grad_attention, out_again, preferred_element_type=jnp.float32
    )
    grad_context = grad_context.astype(jnp.bfloat16).reshape(tiled)
    grad_values = jnp.einsum(
        "rnhqk,rnqhe->rnkhe", probs_low, grad_context, preferred_element_type=jnp.float32
    )
    grad_probs = jnp.einsum(
        "rnqhe,rnkhe->rnhqk", grad_context, value_heads, preferred_element_type=jnp.float32
    )
    probs = jnp.exp(masked_scores() - log_total)
    grad_scores = (
        probs * (grad_probs - jnp.sum(probs * grad_probs, axis=-1, keepdims=True))
    ).astype(jnp.bfloat16)
    grad_queries = (
        jnp.einsum("rnhqk,rnkhe->rnqhe", grad_scores, key_heads, preferred_element_type=jnp.float32)
        * scaling
    )
    grad_keys = (
        jnp.einsum("rnhqk,rnqhe->rnkhe", grad_scores, queries, preferred_element_type=jnp.float32)
        * scaling
    )
    grad_qkv = jnp.concatenate(
        [
            grad_queries.reshape(tokens, model_width),
            grad_keys.reshape(tokens, model_width),
            grad_values.reshape(tokens, model_width),
        ],
        axis=1,
    ).astype(jnp.bfloat16)
    grad_qkv_weight = jnp.einsum("td,te->de", first, grad_qkv, preferred_element_type=jnp.float32)
    grad_query_bias = column_sums(grad_qkv[:, :model_width])
    grad_value_bias = column_sums(grad_qkv[:, 2 * model_width :])
    grad_first = jnp.einsum("te,de->td", grad_qkv, qkv_again, preferred_element_type=jnp.float32)
    grad_in_norm, grad_gain_one, grad_shift_one = norm_back_one(grad_first)
    grad_inputs = (
        (grad_middle + grad_in_norm)
        .astype(jnp.bfloat16)
        .reshape(row_count, slot_count, model_width)
    )
    attn_sums = (
        lax.psum_scatter(grad_gain_one, "fsdp", scatter_dimension=0, tiled=True),
        lax.psum_scatter(grad_shift_one, "fsdp", scatter_dimension=0, tiled=True),
        lax.psum_scatter(grad_qkv_weight, "fsdp", scatter_dimension=0, tiled=True),
        lax.psum_scatter(grad_query_bias, "fsdp", scatter_dimension=0, tiled=True),
        lax.psum_scatter(grad_value_bias, "fsdp", scatter_dimension=0, tiled=True),
        lax.psum_scatter(grad_out, "fsdp", scatter_dimension=0, tiled=True),
        lax.psum_scatter(grad_out_bias, "fsdp", scatter_dimension=0, tiled=True),
    )
    return (
        result,
        grad_inputs,
        attn_sums[0],
        attn_sums[1],
        attn_sums[2],
        attn_sums[3],
        attn_sums[4],
        attn_sums[5],
        attn_sums[6],
        mlp_sums[0],
        mlp_sums[1],
        mlp_sums[2],
        mlp_sums[3],
        mlp_sums[4],
        mlp_sums[5],
    )


def solution(mesh):
    return jax.shard_map(
        shards,
        mesh=mesh,
        in_specs=(
            P("fsdp", None, None),
            P("fsdp", None),
            P("fsdp", None, None),
            P("fsdp"),
            P("fsdp"),
            P("fsdp", None),
            P("fsdp"),
            P("fsdp"),
            P("fsdp", None),
            P("fsdp"),
            P("fsdp"),
            P("fsdp"),
            P("fsdp", None),
            P("fsdp"),
            P("fsdp", None),
            P("fsdp"),
        ),
        out_specs=(
            P("fsdp", None, None),
            P("fsdp", None, None),
            P("fsdp"),
            P("fsdp"),
            P("fsdp", None),
            P("fsdp"),
            P("fsdp"),
            P("fsdp", None),
            P("fsdp"),
            P("fsdp"),
            P("fsdp"),
            P("fsdp", None),
            P("fsdp"),
            P("fsdp", None),
            P("fsdp"),
        ),
        check_vma=False,
    )
```

profile of v0, /device:TPU:0, one launch (start us, length us, event | category | flops | bytes accessed | tf_op | source)
XLA Modules:
  0.0 820.7 jit_solution(5012870485716930246)
XLA Ops:
  7.2 1.7 convert_element_type.139
  9.0 1.5 convert_element_type.149
  10.6 1.6 convert_element_type.157
  12.3 1.6 convert_element_type.161
  14.0 0.7 convert_element_type.134
  14.7 0.7 convert_element_type.136
  19.9 1.6 convert_reduce_fusion.4
  24.2 43.6 %all-reduce.19 = (bf16[768]{0:T(1024)(128)(2,1)S(1)}, bf16[768]{0:T(1024)(128)(2,1)S(1)}, bf16[768]{0:T(1024)(128)(2,1)S(1)}, bf16[768]{0:T(1024)(128)(2,1)S(1)}...) all-reduce(bf16[768]{0:T(1024)(128)(2,1)S(1)} %dynamic-update-slice, ...), channel_id=1, replica_groups=mesh['fsdp'=32] {'fsdp'}, use_global_device_ids=true, to_apply=%add.1 | all-reduce | flops 9216 | bytes 36864
  68.6 0.9 and_or_fusion
  70.1 4.4 all-gather.5.cloned.1.call-done
  74.5 5.5 add_convert_fusion.1
  80.0 1.3 fusion.35
  81.3 3.5 reshape.188
  84.8 3.5 reshape.189
  88.3 4.1 reshape.187
  92.4 6.7 fusion.6
  99.1 2.3 exponential_reduce_fusion
  101.4 2.3 convert_bitcast_fusion.1
  103.8 0.8 copy.59
  104.6 3.4 convert_element_type.148
  108.0 22.8 %all-gather.7.cloned.1.call-done = bf16[768,768]{1,0:T(8,128)(2,1)} async-done(((bf16[24,768]{1,0:T(8,128)(2,1)}), bf16[768,768]{1,0:T(8,128)(2,1)}) %all-gather.7.cloned.1.call-update) | async-done | bytes 1179664 | tf_op jit(solution)/shard_map/all_gather | solution.py:56
  130.8 3.4 fusion.36
  134.7 0.9 copy-done.36
  135.6 61.3 %all-gather.9.cloned.1.call-done = bf16[768,3072]{1,0:T(8,128)(2,1)} async-done(((bf16[24,3072]{1,0:T(8,128)(2,1)}), bf16[768,3072]{1,0:T(8,128)(2,1)}) %all-gather.9.cloned.1.call-update) | async-done | bytes 4718608 | tf_op jit(solution)/shard_map/all_gather | solution.py:109
  196.9 9.4 %fusion.31 = f32[864,3072]{1,0:T(8,128)} fusion(bf16[768,3072]{1,0:T(8,128)(2,1)} %all-gather.9.cloned.1.call-done, f32[864,768]{1,0:T(8,128)S(1)} %get-tuple-element.52, f32[768]{0:T(1024)S(1)} %convert_element_type.155, f32[768]{0:T(1024)S(1)} %convert_element_type.153, f32[864]{0:T(1024)S(1)} %fusion.27, f32[864]{0:T(1024)S(1)} %broadcast_multiply_fusion.1), kind=kOutput, calls=%fused_computation.83 | convolution fusion | flops 4080181248 | bytes 18002688 | tf_op jit(solution)/shard_map/dot_general | solution.py:119
  206.3 55.8 %all-gather.11.cloned.1.call-done = bf16[3072,768]{1,0:T(8,128)(2,1)} async-done(((bf16[96,768]{1,0:T(8,128)(2,1)}), bf16[3072,768]{1,0:T(8,128)(2,1)}) %all-gather.11.cloned.1.call-update) | async-done | bytes 4718608 | tf_op jit(solution)/shard_map/all_gather | solution.py:111
  262.1 33.5 %convert_reduce_fusion = (f32[3072]{0:T(1024)}, bf16[864,3072]{1,0:T(8,128)(2,1)S(1)}, f32[864,3072]{1,0:T(8,128)}) fusion(f32[864,3072]{1,0:T(8,128)} %fusion.31, f32[3072]{0:T(1024)S(1)} %copy-done.28, bf16[864,768]{1,0:T(8,128)(2,1)} %bitcast.51, bf16[3072,768]{1,0:T(8,128)(2,1)} %all-gather.11.cloned.1.call-done), kind=kOutput, calls=%fused_computation.2 | convolution fusion | flops 4275926016 | bytes 32612352 | tf_op jit(solution)/shard_map/td,fd->tf/dot_general | solution.py:143
  295.6 5.3 multiply_reduce_fusion.1
  301.0 1.0 fusion.34
  302.0 1.6 copy-done.7
  303.6 1.1 convert_reduce_fusion.1
  304.6 2.9 fusion.38
  307.6 2.5 convolution_convert_fusion
  310.2 3.7 reshape.193
  313.9 8.1 multiply_reduce_fusion
  322.0 2.1 multiply_convert_fusion.3
  324.1 2.0 fusion.8
  326.2 2.6 copy.64
  328.7 5.7 reshape.194
  334.4 3.7 fusion.9
  338.2 2.6 copy.66
  340.8 5.9 reshape.195
  346.7 4.5 convert_bitcast_fusion
  351.1 0.8 copy.68
  352.0 3.0 reshape.196
  355.0 1.6 constant_dynamic-update-slice_fusion.2
  357.2 1.9 copy-done.25
  359.1 5.9 fusion.37
  365.0 1.7 copy-done.2
  366.8 10.3 %fusion.30 = f32[768,3072]{1,0:T(8,128)} fusion(bf16[864,3072]{1,0:T(8,128)(2,1)} %copy-done.15, f32[864,768]{1,0:T(8,128)S(1)} %copy-done.2, f32[768]{0:T(1024)S(1)} %copy-done.27, f32[768]{0:T(1024)S(1)} %convert_element_type.153, f32[864]{0:T(1024)S(1)} %fusion.27, f32[864]{0:T(1024)S(1)} %broadcast_multiply_fusion.1), kind=kOutput, calls=%fused_computation.82 | convolution fusion | flops 4080181248 | bytes 17412864 | tf_op jit(solution)/shard_map/td,tf->df/dot_general | solution.py:145
  377.7 8.8 %multiply_convert_fusion = bf16[864,3072]{1,0:T(8,128)(2,1)S(1)} fusion(f32[864,3072]{1,0:T(8,128)} %get-tuple-element.41, f32[864,3072]{1,0:T(8,128)} %fusion.31, f32[3072]{0:T(1024)S(1)} %copy-done.29), kind=kLoop, calls=%fused_computation.4 | loop fusion | flops 10616832 | bytes 26554368 | tf_op jit(solution)/shard_map/convert_element_type | solution.py:123
  386.5 2.4 copy-done.16
  389.0 7.7 fusion.39
  397.3 1.7 convert_reduce_fusion.5
  399.0 1.6 convert_reduce_fusion.3
  400.9 8.4 %multiply_reduce_fusion.2 = (f32[768]{0:T(1024)S(1)}, f32[864]{0:T(1024)S(1)}, f32[768]{0:T(1024)S(1)}, f32[864,768]{1,0:T(8,128)}) fusion(f32[864]{0:T(1024)S(1)} %copy-done.33, f32[864]{0:T(1024)S(1)} %copy-done.31, bf16[3,288,768]{2,1,0:T(8,128)(2,1)S(1)} %copy-done.9, f32[768]{0:T(1024)S(1)} %copy-done.35, bf16[864,2304]{1,0:T(8,128)(2,1)} %copy-done.25, ...), kind=kOutput, calls=%fused_computation.39 | convolution fusion | flops 3064944384 | bytes 12848256 | tf_op jit(solution)/shard_map/te,de->td/dot_general | solution.py:206
  409.3 40.5 %all-reduce.18 = (f32[768]{0:T(1024)S(1)}, f32[768]{0:T(1024)S(1)}, f32[768]{0:T(1024)S(1)}, f32[768]{0:T(1024)S(1)}, f32[768]{0:T(1024)S(1)}, /*index=5*/f32[76...) all-reduce(f32[768]{0:T(1024)S(1)} %get-tuple-element.17, ...), channel_id=2, replica_groups=mesh['fsdp'=32] {'fsdp'}, use_global_device_ids=true, to_apply=%region_12.13.clone | all-reduce | flops 9216 | bytes 73728
  454.5 4.3 add_add_fusion
  458.8 2.0 reduce_sum.182
  461.3 5.4 add_convert_fusion.2
  466.7 9.3 %add_convert_fusion.3 = bf16[864,768]{1,0:T(8,128)(2,1)} fusion(f32[864,768]{1,0:T(8,128)S(1)} %copy-done.2, bf16[864,3072]{1,0:T(8,128)(2,1)} %copy-done.16, bf16[3072,768]{1,0:T(8,128)(2,1)} %all-gather.11.cloned.1.call-done, f32[768]{0:T(1024)S(1)} %convert_element_type.163), kind=kOutput, calls=%fused_computation.43 | convolution fusion | flops 4078854144 | bytes 14011392 | tf_op jit(solution)/shard_map/dot_general | solution.py:124
  476.0 54.4 %reduce-scatter.5.cloned.1.call-done = f32[24,2304]{1,0:T(8,128)} async-done(((f32[768,2304]{1,0:T(8,128)}), f32[24,2304]{1,0:T(8,128)}) %reduce-scatter.5.cloned.1.call-update) | async-done | bytes 221200 | tf_op jit(solution)/shard_map/reduce_scatter | solution.py:216
  530.4 141.6 %reduce-scatter.9.cloned.1.call-done = f32[24,3072]{1,0:T(8,128)} async-done(((f32[768,3072]{1,0:T(8,128)}), f32[24,3072]{1,0:T(8,128)}) %reduce-scatter.9.cloned.1.call-update) | async-done | bytes 294928 | tf_op jit(solution)/shard_map/reduce_scatter | solution.py:153
  671.9 141.6 %reduce-scatter.11.cloned.1.call-done = f32[96,768]{1,0:T(8,128)} async-done(((f32[3072,768]{1,0:T(8,128)}), f32[96,768]{1,0:T(8,128)}) %reduce-scatter.11.cloned.1.call-update) | async-done | bytes 294928 | tf_op jit(solution)/shard_map/reduce_scatter | solution.py:155
  (177 shorter events, 17.0 us)
Async XLA Ops:
  7.2 14.5 %copy-start.8 = (bf16[3,288,768]{2,1,0:T(8,128)(2,1)S(1)}, bf16[3,288,768]{2,1,0:T(8,128)(2,1)}, u32[]{:S(2)}) copy-start(bf16[3,288,768]{2,1,0:T(8,128)(2,1)} %param.16) | copy-start | bytes 3981316
  7.2 61.3 %copy-start.42 = (s32[3,288]{1,0:T(4,128)S(1)}, s32[3,288]{1,0:T(4,128)}, u32[]{:S(2)}) copy-start(s32[3,288]{1,0:T(4,128)} %param.17) | copy-start | bytes 10372
  7.2 67.3 %all-gather.5.cloned.1.call-start = ((), (), s32[]{:S(2)}) async-start(), calls=%async_computation.4 | async-start | bytes 3649536 | tf_op jit(solution)/shard_map/all_gather | solution.py:53
  9.0 121.9 %all-gather.7.cloned.1.call-start = ((), (), s32[]{:S(2)}) async-start(), calls=%async_computation.5 | async-start | bytes 1216512 | tf_op jit(solution)/shard_map/all_gather | solution.py:56
  10.5 186.3 %all-gather.9.cloned.1.call-start = ((), (), s32[]{:S(2)}) async-start(), calls=%async_computation.6 | async-start | bytes 4866048 | tf_op jit(solution)/shard_map/all_gather | solution.py:109
  12.3 249.9 %all-gather.11.cloned.1.call-start = ((), (), s32[]{:S(2)}) async-start(), calls=%async_computation.7 | async-start | bytes 4866048 | tf_op jit(solution)/shard_map/all_gather | solution.py:111
  14.0 462.0 %reduce-scatter.7.cloned.1.call-start = ((), (), s32[]{:S(2)}) async-start(), calls=%async_computation.9 | async-start | bytes 2433024 | tf_op jit(solution)/shard_map/reduce_scatter | solution.py:219
  21.6 58.3 %copy-start.30 = (f32[864]{0:T(1024)}, f32[864]{0:T(1024)S(1)}, u32[]{:S(2)}) copy-start(f32[864]{0:T(1024)S(1)} %div.39) | copy-start | bytes 10372
  22.3 45.6 %copy-start.38 = (f32[864]{0:T(1024)}, f32[864]{0:T(1024)S(1)}, u32[]{:S(2)}) copy-start(f32[864]{0:T(1024)S(1)} %add.118) | copy-start | bytes 10372
  22.3 57.7 %copy-start.32 = (f32[864]{0:T(1024)}, f32[864]{0:T(1024)S(1)}, u32[]{:S(2)}) copy-start(f32[864]{0:T(1024)S(1)} %rsqrt.20) | copy-start | bytes 10372
  67.8 12.1 %copy-start.34 = (f32[768]{0:T(1024)}, f32[768]{0:T(1024)S(1)}, u32[]{:S(2)}) copy-start(f32[768]{0:T(1024)S(1)} %convert_element_type.135) | copy-start | bytes 9220
  67.9 129.0 %copy-start.26 = (f32[768]{0:T(1024)}, f32[768]{0:T(1024)S(1)}, u32[]{:S(2)}) copy-start(f32[768]{0:T(1024)S(1)} %convert_element_type.155) | copy-start | bytes 9220
  70.0 4.4 copy-start.22
  92.4 9.0 %copy-start.5 = (bf16[3,8,36,12,64]{4,3,2,1,0:T(8,128)(2,1)}, bf16[3,8,36,12,64]{4,3,2,1,0:T(8,128)(2,1)S(1)}, u32[]{:S(2)}) copy-start(bf16[3,8,36,12,64]{4,3,2,1,0:T(8,128)(2,1)S(1)} %reshape.187) | copy-start | bytes 3981316
  92.4 6.7 copy-start.20
  99.1 4.7 copy-start
  101.4 2.4 copy-start.18
  134.2 166.7 %copy-start.1 = (f32[864,768]{1,0:T(8,128)}, f32[864,768]{1,0:T(8,128)S(1)}, u32[]{:S(2)}) copy-start(f32[864,768]{1,0:T(8,128)S(1)} %get-tuple-element.52) | copy-start | bytes 7962628
  134.7 0.9 copy-start.36
  135.6 126.5 %copy-start.28 = (f32[3072]{0:T(1024)S(1)}, f32[3072]{0:T(1024)}, u32[]{:S(2)}) copy-start(f32[3072]{0:T(1024)} %convert_element_type.159) | copy-start | bytes 36868
  262.1 33.5 %copy-start.46 = (bf16[768,3072]{1,0:T(8,128)(2,1)S(1)}, bf16[768,3072]{1,0:T(8,128)(2,1)}, u32[]{:S(2)}) copy-start(bf16[768,3072]{1,0:T(8,128)(2,1)} %all-gather.9.cloned.1.call-done) | copy-start | bytes 14155780
  295.6 5.3 copy-start.15
  295.6 5.3 copy-start.37
  301.0 2.6 copy-start.10
  302.0 1.6 copy-start.7
  302.0 2.7 copy-start.24
  307.6 222.8 %reduce-scatter.5.cloned.1.call-start = ((), (), s32[]{:S(2)}) async-start(), calls=%async_computation.8 | async-start | bytes 7299072 | tf_op jit(solution)/shard_map/reduce_scatter | solution.py:216
  310.1 3.7 copy-start.19
  310.1 3.7 copy-start.21
  310.2 11.8 %slice-start = ((s8[5898240]{0:T(1024)(128)(4,1)}), s8[1703936]{0:T(1024)(128)(4,1)S(1)}, s32[]{:S(2)}) async-start(s8[5898240]{0:T(1024)(128)(4,1)} %bitcast.47), calls=%async_computation.12 | async-start | bytes 3407872
  313.8 8.1 slice-start.1
  322.0 2.2 copy-start.14
  324.1 2.0 copy-start.3
  328.7 5.7 copy-start.4
  340.8 5.9 copy-start.6
  355.0 1.7 copy-start.17
  355.0 2.1 copy-start.12
  355.0 4.1 copy-start.23
  357.2 1.9 copy-start.25
  365.0 1.8 copy-start.2
  365.0 1.8 copy-start.27
  365.0 306.9 %reduce-scatter.9.cloned.1.call-start = ((), (), s32[]{:S(2)}) async-start(), calls=%async_computation.10 | async-start | bytes 9732096 | tf_op jit(solution)/shard_map/reduce_scatter | solution.py:153
  377.0 0.7 copy-start.29
  377.1 436.5 %reduce-scatter.11.cloned.1.call-start = ((), (), s32[]{:S(2)}) async-start(), calls=%async_computation.11 | async-start | bytes 9732096 | tf_op jit(solution)/shard_map/reduce_scatter | solution.py:155
  377.7 11.2 %copy-start.11 = (bf16[3,288,768]{2,1,0:T(8,128)(2,1)S(1)}, bf16[3,288,768]{2,1,0:T(8,128)(2,1)}, u32[]{:S(2)}) copy-start(bf16[3,288,768]{2,1,0:T(8,128)(2,1)} %param.18) | copy-start | bytes 3981316
  386.5 2.4 copy-start.16
  396.6 0.7 copy-start.45
  396.7 4.2 copy-start.31
  396.7 4.2 copy-start.33
  396.7 4.2 copy-start.35
  396.7 3.9 copy-start.13
  396.7 4.1 copy-start.9
  400.9 8.5 %copy-start.40 = (f32[768]{0:T(1024)S(1)}, f32[768]{0:T(1024)}, u32[]{:S(2)}) copy-start(f32[768]{0:T(1024)} %get-tuple-element.42) | copy-start | bytes 9220
  400.9 8.4 %copy-start.41 = (f32[3072]{0:T(1024)S(1)}, f32[3072]{0:T(1024)}, u32[]{:S(2)}) copy-start(f32[3072]{0:T(1024)} %get-tuple-element.39) | copy-start | bytes 36868
  400.9 8.4 %copy-start.43 = (f32[768]{0:T(1024)S(1)}, f32[768]{0:T(1024)}, u32[]{:S(2)}) copy-start(f32[768]{0:T(1024)} %get-tuple-element.15) | copy-start | bytes 9220
  400.9 8.4 %copy-start.44 = (f32[768]{0:T(1024)S(1)}, f32[768]{0:T(1024)}, u32[]{:S(2)}) copy-start(f32[768]{0:T(1024)} %get-tuple-element.19) | copy-start | bytes 9220
  400.9 53.6 %copy-start.39 = (f32[864]{0:T(1024)S(1)}, f32[864]{0:T(1024)}, u32[]{:S(2)}) copy-start(f32[864]{0:T(1024)} %copy-done.38) | copy-start | bytes 10372
Sparse Core Ops, SparseCore 0:
  11.5 62.9 all-gather.4
  78.0 52.8 all-gather.6
  134.3 62.4 all-gather.8
  200.2 61.9 all-gather.10
  307.7 97.9 reduce-scatter.6
  411.8 118.5 reduce-scatter.4
  536.8 135.0 reduce-scatter.8
  678.4 135.1 reduce-scatter.10
where the time goes:
time: 825 us; the launch traced here: 821 us
  waiting for transfers between devices  482 us (58%)
  matrix products  131 us (16%)
  blocking collectives  84.1 us (10%)
  local copies, waits for them, and re-layouts  60.3 us (7%)
  other arithmetic  47.5 us (6%)
  between operations  15.2 us (2%)
    reduce_scatter x1, waiting for transfers between devices, shards(): lax.psum_scatter(grad_down, 'fsdp', scatter_dimension=0, tiled=True)  142 us
    reduce_scatter x1, waiting for transfers between devices, shards(): lax.psum_scatter(grad_up, 'fsdp', scatter_dimension=0, tiled=True)  142 us
    unnamed x2, blocking collectives  84.1 us
    all_gather x1, waiting for transfers between devices, shards(): lax.all_gather(w_up.astype(jnp.bfloat16), 'fsdp', axis=0, tiled=True)  61.3 us
    all_gather x1, waiting for transfers between devices, shards(): lax.all_gather(w_down.astype(jnp.bfloat16), 'fsdp', axis=0, tiled=True)  55.8 us
    reduce_scatter x1, waiting for transfers between devices, shards(): lax.psum_scatter(grad_qkv_weight, 'fsdp', scatter_dimension=0, tiled=True)  54.4 us
    dot_general x1, matrix products, shards(): jnp.einsum('td,fd->tf', grad_branch, down_again, preferred_element_type=j...  33.5 us
    all_gather x1, waiting for transfers between devices, shards(): lax.all_gather(w_out.astype(jnp.bfloat16), 'fsdp', axis=0, tiled=True)  22.8 us
  transfers between devices with their start and end apart: 8, of which 7 were waited for; matrix products, arithmetic and copies ran while one was open for 22% of the time, Pallas kernels for 0%

commit v1 on v0

--- a/solution.py
+++ b/solution.py
@@ -6,6 +6,27 @@
 HEAD_DIM = 64
 PATCHES = 36
 EPSILON = 1e-06
+
+
+def laid_out(blocks, dim):
+    shape = list(blocks.shape[1:])
+    shape[dim] *= blocks.shape[0]
+    return jnp.moveaxis(blocks, 0, dim).reshape(shape)
+
+
+def collected_by_bits(shard, axis):
+    count, mine = (lax.axis_size(axis), lax.axis_index(axis))
+    tiles, apart = (shard[None], 1)
+    while apart < count:
+        other = lax.ppermute(tiles, axis, [(i, i ^ apart) for i in range(count)])
+        low = mine & apart == 0
+        tiles = jnp.concatenate([jnp.where(low, tiles, other), jnp.where(low, other, tiles)])
+        apart *= 2
+    return tiles
+
+
+def doubled_up(shard, axis, dim):
+    return laid_out(collected_by_bits(shard, axis), dim)
 
 
 def norm_layer(value, gain, shift):
@@ -108,7 +129,7 @@
         lax.all_gather(mid_shift.astype(jnp.bfloat16), "fsdp", axis=0, tiled=True),
         lax.all_gather(w_up.astype(jnp.bfloat16), "fsdp", axis=0, tiled=True),
         lax.all_gather(b_up.astype(jnp.bfloat16), "fsdp", axis=0, tiled=True),
-        lax.all_gather(w_down.astype(jnp.bfloat16), "fsdp", axis=0, tiled=True),
+        doubled_up(w_down.astype(jnp.bfloat16), "fsdp", 0),
         lax.all_gather(b_down.astype(jnp.bfloat16), "fsdp", axis=0, tiled=True),
     )
     gain_two, shift_two, up_weight, up_bias, down_weight, down_bias = mlp_full

time: 825 us -> 920 us (1.12)
  waiting for transfers between devices: 482 us -> 543 us
  other arithmetic: 47.5 us -> 62.1 us
  local copies, waits for them, and re-layouts: 60.3 us -> 73.7 us
    ppermute x0 -> x5, waiting for transfers between devices: none -> 175 us  [collected_by_bits(): other = lax.ppermute(tiles, axis, [(i, i ^ apart) for i in range(count)])]
    reduce_scatter x1, waiting for transfers between devices: 142 us -> 83.9 us  [shards(): lax.psum_scatter(grad_up, 'fsdp', scatter_dimension=0, tiled=True)]
    reduce_scatter x1, waiting for transfers between devices: 54.4 us -> 0.01 us  [shards(): lax.psum_scatter(grad_qkv_weight, 'fsdp', scatter_dimension=0, tiled=True)]
    unnamed x127 -> x123, local copies, waits for them, and re-layouts: 19.2 us -> 22.9 us
  transfers between devices with their start and end apart: 8 -> 13, of which waited for: 7 -> 11; matrix products, arithmetic and copies ran while one was open for 22% -> 21% of each run, Pallas kernels for 0% -> 0%
where the time goes in v1:
time: 920 us; the launch traced here: 916 us
  waiting for transfers between devices  543 us (59%)
  matrix products  132 us (14%)
  blocking collectives  82.5 us (9%)
  local copies, waits for them, and re-layouts  73.7 us (8%)
  other arithmetic  62.1 us (7%)
  between operations  15 us (2%)
    ppermute x5, waiting for transfers between devices, collected_by_bits(): other = lax.ppermute(tiles, axis, [(i, i ^ apart) for i in range(count)])  175 us
    reduce_scatter x1, waiting for transfers between devices, shards(): lax.psum_scatter(grad_down, 'fsdp', scatter_dimension=0, tiled=True)  142 us
    reduce_scatter x1, waiting for transfers between devices, shards(): lax.psum_scatter(grad_up, 'fsdp', scatter_dimension=0, tiled=True)  83.9 us
    unnamed x2, blocking collectives  82.5 us
    all_gather x1, waiting for transfers between devices, shards(): lax.all_gather(w_up.astype(jnp.bfloat16), 'fsdp', axis=0, tiled=True)  62.1 us
    all_gather x1, waiting for transfers between devices, shards(): lax.all_gather(w_down.astype(jnp.bfloat16), 'fsdp', axis=0, tiled=True)  55.8 us
    dot_general x1, matrix products, shards(): jnp.einsum('td,fd->tf', grad_branch, down_again, preferred_element_type=j...  33.8 us
    unnamed x123, local copies, waits for them, and re-layouts  22.9 us
  transfers between devices with their start and end apart: 13, of which 11 were waited for; matrix products, arithmetic and copies ran while one was open for 21% of the time, Pallas kernels for 0%

profile of v1, /device:TPU:0, one launch (start us, length us, event | category | flops | bytes accessed | tf_op | source)
XLA Modules:
  0.0 915.5 jit_solution(4699305314801459004)
XLA Ops:
  7.2 1.7 convert_element_type.139
  9.0 1.5 convert_element_type.149
  10.6 1.6 convert_element_type.157
  12.3 1.6 convert_element_type.161
  21.8 43.3 %all-reduce.19 = (bf16[768]{0:T(1024)(128)(2,1)S(1)}, bf16[768]{0:T(1024)(128)(2,1)S(1)}, bf16[768]{0:T(1024)(128)(2,1)S(1)}, bf16[768]{0:T(1024)(128)(2,1)S(1)}...) all-reduce(bf16[768]{0:T(1024)(128)(2,1)S(1)} %dynamic-update-slice, ...), channel_id=1, replica_groups=mesh['fsdp'=32] {'fsdp'}, use_global_device_ids=true, to_apply=%add.1 | all-reduce | flops 9216 | bytes 36864
  65.1 1.6 convert_reduce_fusion.4
  70.2 4.6 all-gather.5.cloned.1.call-done
  74.8 5.5 add_convert_fusion.1
  80.3 2.1 fusion.35
  82.4 4.1 reshape.190
  86.5 5.5 reshape.192
  92.0 5.2 reshape.191
  97.2 5.4 fusion.6
  102.7 2.3 exponential_reduce_fusion
  105.2 2.5 convert_bitcast_fusion.1
  108.6 3.0 convert_element_type.148
  111.6 19.5 %all-gather.7.cloned.1.call-done = bf16[768,768]{1,0:T(8,128)(2,1)} async-done(((bf16[24,768]{1,0:T(8,128)(2,1)}), bf16[768,768]{1,0:T(8,128)(2,1)}) %all-gather.7.cloned.1.call-update) | async-done | bytes 1179664 | tf_op jit(solution)/shard_map/all_gather | solution.py:77
  131.0 3.4 fusion.36
  134.9 62.1 %all-gather.9.cloned.1.call-done = bf16[768,3072]{1,0:T(8,128)(2,1)} async-done(((bf16[24,3072]{1,0:T(8,128)(2,1)}), bf16[768,3072]{1,0:T(8,128)(2,1)}) %all-gather.9.cloned.1.call-update) | async-done | bytes 4718608 | tf_op jit(solution)/shard_map/all_gather | solution.py:130
  197.0 9.5 %fusion.31 = f32[864,3072]{1,0:T(8,128)} fusion(bf16[768,3072]{1,0:T(8,128)(2,1)} %all-gather.9.cloned.1.call-done, f32[864,768]{1,0:T(8,128)S(1)} %get-tuple-element.62, f32[768]{0:T(1024)S(1)} %convert_element_type.155, f32[768]{0:T(1024)S(1)} %convert_element_type.153, f32[864]{0:T(1024)S(1)} %fusion.27, f32[864]{0:T(1024)S(1)} %broadcast_multiply_fusion.1), kind=kOutput, calls=%fused_computation.98 | convolution fusion | flops 4080181248 | bytes 18002688 | tf_op jit(solution)/shard_map/dot_general | solution.py:140
  206.5 55.8 %all-gather.11.cloned.1.call-done = bf16[3072,768]{1,0:T(8,128)(2,1)} async-done(((bf16[96,768]{1,0:T(8,128)(2,1)}), bf16[3072,768]{1,0:T(8,128)(2,1)}) %all-gather.11.cloned.1.call-update) | async-done | bytes 4718608 | tf_op jit(solution)/shard_map/all_gather | solution.py:154
  262.3 33.8 %convert_reduce_fusion = (f32[3072]{0:T(1024)}, bf16[864,3072]{1,0:T(8,128)(2,1)S(1)}, f32[864,3072]{1,0:T(8,128)}) fusion(f32[864,3072]{1,0:T(8,128)} %fusion.31, f32[3072]{0:T(1024)S(1)} %copy-done.30, bf16[864,768]{1,0:T(8,128)(2,1)} %bitcast.54, bf16[3072,768]{1,0:T(8,128)(2,1)} %all-gather.11.cloned.1.call-done), kind=kOutput, calls=%fused_computation.2 | convolution fusion | flops 4275926016 | bytes 32612352 | tf_op jit(solution)/shard_map/td,fd->tf/dot_general | solution.py:164
  296.2 5.3 multiply_reduce_fusion.1
  305.6 2.8 fusion.38
  308.4 4.0 convolution_convert_fusion
  312.3 5.3 reshape.197
  317.6 10.2 %multiply_reduce_fusion = (f32[3,8,12,36]{3,2,1,0:T(8,128)S(1)}, f32[3,8,12,36,36]{3,4,2,1,0:T(8,128)}) fusion(f32[3,8,12,36,36]{3,4,2,1,0:T(8,128)} %copy-done, f32[3,8,12,36]{3,2,1,0:T(8,128)S(1)} %copy-done.17, pred[3,8,36,36]{2,3,1,0:T(8,128)(4,1)S(1)} %copy-done.19, bf16[3,8,36,12,64]{4,3,2,1,0:T(8,128)(2,1)} %copy-done.2, ...), kind=kOutput, calls=%fused_computation.22 | convolution fusion | flops 49631616 | bytes 5754240 | tf_op jit(solution)/shard_map/rnqhe,rnkhe->rnhqk/dot_general | solution.py:201
  327.9 5.9 multiply_convert_fusion.3
  333.8 2.0 fusion.8
  335.8 2.7 copy.64
  338.5 5.5 reshape.198
  344.1 4.7 fusion.9
  348.7 2.6 copy.66
  351.3 5.5 reshape.199
  356.9 5.5 convert_bitcast_fusion
  362.4 2.6 copy.68
  365.1 5.5 reshape.200
  370.6 1.6 constant_dynamic-update-slice_fusion.2
  372.8 2.0 copy-done.26
  374.8 6.0 fusion.37
  381.4 10.6 %fusion.30 = f32[768,3072]{1,0:T(8,128)} fusion(bf16[864,3072]{1,0:T(8,128)(2,1)} %copy-done.12, f32[864,768]{1,0:T(8,128)S(1)} %get-tuple-element.62, f32[768]{0:T(1024)S(1)} %copy-done.29, f32[768]{0:T(1024)S(1)} %convert_element_type.153, f32[864]{0:T(1024)S(1)} %fusion.27, f32[864]{0:T(1024)S(1)} %broadcast_multiply_fusion.1), kind=kOutput, calls=%fused_computation.97 | convolution fusion | flops 4080181248 | bytes 17412864 | tf_op jit(solution)/shard_map/td,tf->df/dot_general | solution.py:166
  392.1 8.6 multiply_convert_fusion
  400.7 2.4 copy-done.14
  403.1 7.7 fusion.39
  414.8 7.9 collective-permute-done.1
  426.1 13.5 %collective-permute-done.2 = bf16[4,96,768]{2,1,0:T(8,128)(2,1)} collective-permute-done((bf16[4,96,768]{2,1,0:T(8,128)(2,1)}, bf16[4,96,768]{2,1,0:T(8,128)(2,1)}, u32[]{:S(2)}, u32[]{:S(2)}) %collective-permute-start.2) | collective-permute-done | bytes 589856 | tf_op jit(solution)/shard_map/ppermute | solution.py:21
  444.2 25.4 %collective-permute-done.3 = bf16[8,96,768]{2,1,0:T(8,128)(2,1)} collective-permute-done((bf16[8,96,768]{2,1,0:T(8,128)(2,1)}, bf16[8,96,768]{2,1,0:T(8,128)(2,1)}, u32[]{:S(2)}, u32[]{:S(2)}) %collective-permute-start.3) | collective-permute-done | bytes 1179680 | tf_op jit(solution)/shard_map/ppermute | solution.py:21
  469.6 1.6 broadcast_select_fusion.3
  472.2 1.6 pad_maximum_fusion.1
  473.9 1.9 collective-permute-start.4
  475.7 1.6 convert_reduce_fusion.5
  477.3 127.7 %collective-permute-done.4 = bf16[16,96,768]{2,1,0:T(8,128)(2,1)} collective-permute-done((bf16[16,96,768]{2,1,0:T(8,128)(2,1)}, bf16[16,96,768]{2,1,0:T(8,128)(2,1)}, u32[]{:S(2)}, u32[]{:S(2)}) %collective-permute-start.4) | collective-permute-done | bytes 2359328 | tf_op jit(solution)/shard_map/ppermute | solution.py:21
  605.0 2.6 broadcast_select_fusion.1
  607.7 2.8 pad_maximum_fusion
  613.0 3.9 multiply_reduce_fusion.2
  616.9 2.2 add_add_fusion
  619.1 2.0 reduce_sum.182
  621.1 1.6 convert_reduce_fusion.3
  622.7 1.6 convert_reduce_fusion.2
  624.3 39.3 %all-reduce.18 = (f32[768]{0:T(1024)S(1)}, f32[768]{0:T(1024)S(1)}, f32[768]{0:T(1024)S(1)}, f32[768]{0:T(1024)S(1)}, f32[768]{0:T(1024)S(1)}, /*index=5*/f32[76...) all-reduce(f32[768]{0:T(1024)S(1)} %get-tuple-element.17, ...), channel_id=2, replica_groups=mesh['fsdp'=32] {'fsdp'}, use_global_device_ids=true, to_apply=%region_12.13.clone | all-reduce | flops 9216 | bytes 73728
  668.8 4.8 add_convert_fusion.2
  673.6 9.3 %add_convert_fusion.3 = bf16[864,768]{1,0:T(8,128)(2,1)} fusion(f32[864,768]{1,0:T(8,128)S(1)} %get-tuple-element.62, bf16[864,3072]{1,0:T(8,128)(2,1)} %copy-done.14, bf16[3072,768]{1,0:T(8,128)(2,1)} %bitcast.56, f32[768]{0:T(1024)S(1)} %convert_element_type.163), kind=kOutput, calls=%fused_computation.44 | convolution fusion | flops 4078854144 | bytes 14011392 | tf_op jit(solution)/shard_map/dot_general | solution.py:145
  682.9 83.9 %reduce-scatter.9.cloned.1.call-done = f32[24,3072]{1,0:T(8,128)} async-done(((f32[768,3072]{1,0:T(8,128)}), f32[24,3072]{1,0:T(8,128)}) %reduce-scatter.9.cloned.1.call-update) | async-done | bytes 294928 | tf_op jit(solution)/shard_map/reduce_scatter | solution.py:174
  766.8 141.7 %reduce-scatter.11.cloned.1.call-done = f32[96,768]{1,0:T(8,128)} async-done(((f32[3072,768]{1,0:T(8,128)}), f32[96,768]{1,0:T(8,128)}) %reduce-scatter.11.cloned.1.call-update) | async-done | bytes 294928 | tf_op jit(solution)/shard_map/reduce_scatter | solution.py:176
  (193 shorter events, 39.2 us)
Async XLA Ops:
  7.2 59.6 %copy-start.4 = (bf16[3,288,768]{2,1,0:T(8,128)(2,1)S(1)}, bf16[3,288,768]{2,1,0:T(8,128)(2,1)}, u32[]{:S(2)}) copy-start(bf16[3,288,768]{2,1,0:T(8,128)(2,1)} %param.16) | copy-start | bytes 3981316
  7.2 60.8 %copy-start.42 = (s32[3,288]{1,0:T(4,128)S(1)}, s32[3,288]{1,0:T(4,128)}, u32[]{:S(2)}) copy-start(s32[3,288]{1,0:T(4,128)} %param.17) | copy-start | bytes 10372
  7.2 67.6 %all-gather.5.cloned.1.call-start = ((), (), s32[]{:S(2)}) async-start(), calls=%async_computation.4 | async-start | bytes 3649536 | tf_op jit(solution)/shard_map/all_gather | solution.py:74
  9.0 122.1 %all-gather.7.cloned.1.call-start = ((), (), s32[]{:S(2)}) async-start(), calls=%async_computation.5 | async-start | bytes 1216512 | tf_op jit(solution)/shard_map/all_gather | solution.py:77
  10.5 186.5 %all-gather.9.cloned.1.call-start = ((), (), s32[]{:S(2)}) async-start(), calls=%async_computation.6 | async-start | bytes 4866048 | tf_op jit(solution)/shard_map/all_gather | solution.py:130
  12.3 250.1 %all-gather.11.cloned.1.call-start = ((), (), s32[]{:S(2)}) async-start(), calls=%async_computation.7 | async-start | bytes 4866048 | tf_op jit(solution)/shard_map/all_gather | solution.py:154
  14.0 668.9 %reduce-scatter.7.cloned.1.call-start = ((), (), s32[]{:S(2)}) async-start(), calls=%async_computation.9 | async-start | bytes 2433024 | tf_op jit(solution)/shard_map/reduce_scatter | solution.py:240
  65.0 15.2 %copy-start.31 = (f32[768]{0:T(1024)}, f32[768]{0:T(1024)S(1)}, u32[]{:S(2)}) copy-start(f32[768]{0:T(1024)S(1)} %convert_element_type.135) | copy-start | bytes 9220
  66.8 13.5 %copy-start.33 = (f32[864]{0:T(1024)}, f32[864]{0:T(1024)S(1)}, u32[]{:S(2)}) copy-start(f32[864]{0:T(1024)S(1)} %div.39) | copy-start | bytes 10372
  67.4 0.6 copy-start.39
  67.4 12.9 %copy-start.35 = (f32[864]{0:T(1024)}, f32[864]{0:T(1024)S(1)}, u32[]{:S(2)}) copy-start(f32[864]{0:T(1024)S(1)} %rsqrt.20) | copy-start | bytes 10372
  68.1 128.9 %copy-start.28 = (f32[768]{0:T(1024)}, f32[768]{0:T(1024)S(1)}, u32[]{:S(2)}) copy-start(f32[768]{0:T(1024)S(1)} %convert_element_type.155) | copy-start | bytes 9220
  70.2 10.1 %copy-start.22 = (bf16[864,768]{1,0:T(8,128)(2,1)}, bf16[864,768]{1,0:T(8,128)(2,1)S(1)}, u32[]{:S(2)}) copy-start(bf16[864,768]{1,0:T(8,128)(2,1)S(1)} %add_convert_fusion.5) | copy-start | bytes 3981316
  86.5 18.5 %copy-start.2 = (bf16[3,8,36,12,64]{4,3,2,1,0:T(8,128)(2,1)}, bf16[3,8,36,12,64]{4,3,2,1,0:T(8,128)(2,1)S(1)}, u32[]{:S(2)}) copy-start(bf16[3,8,36,12,64]{4,3,2,1,0:T(8,128)(2,1)S(1)} %reshape.190) | copy-start | bytes 3981316
  97.2 5.4 copy-start.18
  102.7 2.5 copy-start
  105.2 2.5 copy-start.16
  134.8 71.7 %copy-start.37 = (f32[864]{0:T(1024)}, f32[864]{0:T(1024)S(1)}, u32[]{:S(2)}) copy-start(f32[864]{0:T(1024)S(1)} %multiply_reduce_fusion.5) | copy-start | bytes 10372
  134.9 127.4 %copy-start.30 = (f32[3072]{0:T(1024)S(1)}, f32[3072]{0:T(1024)}, u32[]{:S(2)}) copy-start(f32[3072]{0:T(1024)} %convert_element_type.159) | copy-start | bytes 36868
  262.3 33.9 %copy-start.45 = (bf16[768,3072]{1,0:T(8,128)(2,1)S(1)}, bf16[768,3072]{1,0:T(8,128)(2,1)}, u32[]{:S(2)}) copy-start(bf16[768,3072]{1,0:T(8,128)(2,1)} %all-gather.9.cloned.1.call-done) | copy-start | bytes 14155780
  296.2 5.3 copy-start.12
  296.2 5.3 copy-start.38
  301.5 2.5 copy-start.6
  302.5 1.5 copy-start.3
  302.5 3.0 copy-start.24
  304.5 1.1 copy-start.25
  312.3 5.3 copy-start.17
  312.3 5.3 copy-start.19
  327.8 355.1 %reduce-scatter.5.cloned.1.call-start = ((), (), s32[]{:S(2)}) async-start(), calls=%async_computation.8 | async-start | bytes 7299072 | tf_op jit(solution)/shard_map/reduce_scatter | solution.py:237
  327.9 5.9 copy-start.9
  333.8 2.0 copy-start.1
  370.6 1.7 copy-start.15
  370.6 2.1 copy-start.8
  372.3 2.5 copy-start.23
  372.8 2.0 copy-start.26
  380.8 0.7 copy-start.29
  380.8 386.0 %reduce-scatter.9.cloned.1.call-start = ((), (), s32[]{:S(2)}) async-start(), calls=%async_computation.10 | async-start | bytes 9732096 | tf_op jit(solution)/shard_map/reduce_scatter | solution.py:174
  392.1 516.4 %reduce-scatter.11.cloned.1.call-start = ((), (), s32[]{:S(2)}) async-start(), calls=%async_computation.11 | async-start | bytes 9732096 | tf_op jit(solution)/shard_map/reduce_scatter | solution.py:176
  392.1 11.0 %copy-start.7 = (bf16[3,288,768]{2,1,0:T(8,128)(2,1)S(1)}, bf16[3,288,768]{2,1,0:T(8,128)(2,1)}, u32[]{:S(2)}) copy-start(bf16[3,288,768]{2,1,0:T(8,128)(2,1)} %param.18) | copy-start | bytes 3981316
  400.7 2.4 copy-start.14
  410.8 1.0 copy-start.21
  411.8 1.4 collective-permute-start
  413.3 9.4 %collective-permute-start.1 = (bf16[2,96,768]{2,1,0:T(8,128)(2,1)S(1)}, bf16[2,96,768]{2,1,0:T(8,128)(2,1)}, u32[]{:S(2)}, u32[]{:S(2)}) collective-permute-start(bf16[2,96,768]{2,1,0:T(8,128)(2,1)S(1)} %pad_maximum_fusion.4), channel_id=1, source_target_pairs={{0,2},{1,3},{2,0},{3,1},{4,6},{5,7},{6,4},{7,5},{8,10},{9,11},{10,... | collective-permute-start | bytes 884744 | tf_op jit(solution)/shard_map/ppermute | solution.py:21
  423.7 2.4 copy-start.20
  424.6 15.0 %collective-permute-start.2 = (bf16[4,96,768]{2,1,0:T(8,128)(2,1)}, bf16[4,96,768]{2,1,0:T(8,128)(2,1)}, u32[]{:S(2)}, u32[]{:S(2)}) collective-permute-start(bf16[4,96,768]{2,1,0:T(8,128)(2,1)} %pad_maximum_fusion.3), channel_id=1, source_target_pairs={{0,4},{1,5},{2,6},{3,7},{4,0},{5,1},{6,2},{7,3},{8,12},{9,13},{10,... | collective-permute-start | bytes 1769480 | tf_op jit(solution)/shard_map/ppermute | solution.py:21
  440.9 0.8 copy-start.13
  442.8 26.8 %collective-permute-start.3 = (bf16[8,96,768]{2,1,0:T(8,128)(2,1)}, bf16[8,96,768]{2,1,0:T(8,128)(2,1)}, u32[]{:S(2)}, u32[]{:S(2)}) collective-permute-start(bf16[8,96,768]{2,1,0:T(8,128)(2,1)} %pad_maximum_fusion.2), channel_id=1, source_target_pairs={{0,8},{1,9},{2,10},{3,11},{4,12},{5,13},{6,14},{7,15},{8,0},{9,1},... | collective-permute-start | bytes 3538952 | tf_op jit(solution)/shard_map/ppermute | solution.py:21
  471.2 1.0 copy-start.10
  471.2 2.7 copy-start.11
  471.2 4.5 copy-start.44
  473.9 131.1 %collective-permute-start.4 = (bf16[16,96,768]{2,1,0:T(8,128)(2,1)}, bf16[16,96,768]{2,1,0:T(8,128)(2,1)}, u32[]{:S(2)}, u32[]{:S(2)}) collective-permute-start(bf16[16,96,768]{2,1,0:T(8,128)(2,1)} %pad_maximum_fusion.1), channel_id=1, source_target_pairs={{0,16},{1,17},{2,18},{3,19},{4,20},{5,21},{6,22},{7,23},{8,24},{9,... | collective-permute-start | bytes 7077896 | tf_op jit(solution)/shard_map/ppermute | solution.py:21
  607.6 2.9 copy-start.5
  607.6 4.3 copy-start.27
  607.6 4.3 copy-start.32
  607.7 4.3 copy-start.34
  607.7 4.3 copy-start.36
  607.7 5.4 copy-start.46
  613.0 3.9 copy-start.40
  619.1 5.2 copy-start.41
  619.1 5.2 copy-start.43
Sparse Core Ops, SparseCore 0:
  11.5 63.2 all-gather.4
  78.3 52.7 all-gather.6
  134.5 62.4 all-gather.8
  200.4 61.9 all-gather.10
  327.9 97.9 reduce-scatter.6
  432.0 192.9 reduce-scatter.4
  631.5 135.2 reduce-scatter.8
  773.2 135.1 reduce-scatter.10
